TPU v7x, 32 devices: a whole 2x2x4 slice. The times are simulated.
32 devices in a mesh: groups: 2 (over x), seq: 16 (over z, y, core).
Axes of the slice: x: 2, y: 2, z: 4, core: 2. Of those that a mesh axis runs over, the one named last changes fastest.
Arguments:
- images: bfloat16 [4, 2048, 3072], P('groups', 'seq'), parts along dimension 0, may hold values from -6 to 6
- w_qkv: bfloat16 [3072, 1152], replicated, may hold values from -0.109375 to 0.109375
- b_qkv: float32 [1152], replicated, may hold values from -3 to 3
- q_gain: float32 [128], replicated, may hold values from 0.5 to 2.5
- k_gain: float32 [128], replicated, may hold values from 0.5 to 2.5
- key_basis: float32 [3, 128, 32], replicated, may hold values from -0.5 to 0.5
- value_basis: float32 [3, 128, 32], replicated, may hold values from -0.5 to 0.5
- centers: float32 [4, 2, 3, 128], P('groups'), parts along dimension 0, may hold values from -22 to 22
- refresh: int32 [2, 3], replicated, may hold values 0 or 1
- w_out: bfloat16 [384, 3072], replicated, may hold values from -0.3125 to 0.3125
Outputs:
- mixed: bfloat16 [4, 2048, 3072], P('groups', 'seq'), parts along dimension 0
- new_centers: float32 [4, 2, 3, 128], P('groups'), parts along dimension 0
There are 2 independent parts, one for each index of `groups`. A program takes and returns all parts, laid end to end along the dimension named above; an argument that names none is the same for every part. Nothing has to cross between parts.
All inputs are finite; a program needn't handle non-finite values.
Results may differ from a plain program's by a relative error of at most 0.0051.
Values may be sent and summed in bfloat16 or wider, within the bound.
A program may use at most 64 MiB of HBM per device.

v0:
```python
import math
import jax
import jax.numpy as jnp
from jax import lax
from jax.sharding import PartitionSpec as P

epsilon = 1e-06
highest = lax.Precision.HIGHEST


def normalize(values, gain):
    mean_square = jnp.mean(values * values, axis=-1, keepdims=True)
    return values * lax.rsqrt(mean_square + epsilon) * gain


def per_device(
    images, w_qkv, b_qkv, q_gain, k_gain, key_basis, value_basis, centers, refresh, w_out
):
    sample_count, tokens_dev, model_width = images.shape
    head_count, head_dim, code_rank = key_basis.shape
    seq_count = lax.axis_size("seq")
    first_row = lax.axis_index("seq") * tokens_dev
    factor = 1.0 / math.sqrt(head_dim)
    flat_images = images.reshape(sample_count * tokens_dev, model_width)
    projected = jnp.dot(flat_images, w_qkv, preferred_element_type=jnp.float32) + b_qkv
    projected = projected.reshape(sample_count, tokens_dev, 3, head_count, head_dim)
    queries = normalize(projected[:, :, 0], q_gain)
    keys_local = normalize(projected[:, :, 1], k_gain)
    values_local = projected[:, :, 2]
    key_center = centers[:, 0]
    value_center = centers[:, 1]
    key_codes = jnp.einsum(
        "bthd,hdr->bthr", keys_local - key_center[:, None], key_basis, precision=highest
    ).astype(jnp.bfloat16)
    value_codes = jnp.einsum(
        "bthd,hdr->bthr", values_local - value_center[:, None], value_basis, precision=highest
    ).astype(jnp.bfloat16)
    local_sums = jnp.stack([jnp.sum(keys_local, axis=1), jnp.sum(values_local, axis=1)], axis=1)
    summed = lax.psum(local_sums, "seq")
    fresh_means = summed / (tokens_dev * seq_count)
    new_centers = jnp.where(refresh[None, :, :, None] == 1, fresh_means, centers)
    query_heads = queries.transpose(0, 2, 1, 3)
    key_heads = keys_local.transpose(0, 2, 1, 3)
    value_heads = values_local.transpose(0, 2, 1, 3)
    near_scores = jnp.einsum("bhqd,bhsd->bhqs", query_heads, key_heads, precision=highest) * factor
    start_max = jnp.max(near_scores, axis=-1)
    near_weights = jnp.exp(near_scores - start_max[..., None])
    start_sum = jnp.sum(near_weights, axis=-1)
    start_weighted = jnp.einsum("bhqs,bhsd->bhqd", near_weights, value_heads, precision=highest)
    packed = jnp.stack([key_codes, value_codes], axis=2)
    packed = packed.transpose(1, 0, 2, 3, 4).reshape(
        tokens_dev, sample_count, 2 * head_count * code_rank
    )

    def absorb(running, code_block, owned, low_sample, high_sample):
        row_max, row_sum, weighted = running
        block_values = code_block.astype(jnp.float32)
        key_part = block_values[:, :, 0]
        value_part = block_values[:, :, 1]
        key_rebuilt = (
            jnp.einsum("sbhr,hdr->bhsd", key_part, key_basis, precision=highest)
            + key_center[low_sample:high_sample, :, None, :]
        )
        scores = jnp.einsum("bhqd,bhsd->bhqs", query_heads, key_rebuilt, precision=highest) * factor
        scores = jnp.where(owned[None, None, None, :], -jnp.inf, scores)
        new_max = jnp.maximum(row_max, jnp.max(scores, axis=-1))
        fading = jnp.exp(row_max - new_max)
        weights = jnp.exp(scores - new_max[..., None])
        weight_sum = jnp.sum(weights, axis=-1)
        value_rebuilt = (
            jnp.einsum("sbhr,hdr->bhsd", value_part, value_basis, precision=highest)
            + value_center[low_sample:high_sample, :, None, :]
        )
        addition = jnp.einsum("bhqs,bhsd->bhqd", weights, value_rebuilt, precision=highest)
        return (new_max, row_sum * fading + weight_sum, weighted * fading[..., None] + addition)

    start_state = (start_max, start_sum, start_weighted)
    whole_codes = packed.reshape(tokens_dev, sample_count * 2 * head_count * code_rank)
    shard_codes = lax.all_gather(whole_codes, "seq", axis=0, tiled=True)
    row_count = shard_codes.shape[0]
    code_block = shard_codes.reshape(row_count, sample_count - 0, 2, head_count, code_rank)
    positions = jnp.arange(row_count, dtype=jnp.int32)
    owned = (positions >= first_row) & (positions < first_row + tokens_dev)
    block_rows = 512
    block_count = row_count // block_rows

    def advance(inner, blocks):
        return (absorb(inner, blocks[0], blocks[1], 0, sample_count), None)

    stacked = (
        code_block.reshape(block_count, block_rows, sample_count - 0, 2, head_count, code_rank),
        owned.reshape(block_count, block_rows),
    )
    result, unused = lax.scan(advance, start_state, stacked)
    final_max, final_sum, final_weighted = result
    attended = (final_weighted / final_sum[..., None]).transpose(0, 2, 1, 3)
    attended = attended.reshape(sample_count * tokens_dev, head_count * head_dim).astype(
        jnp.bfloat16
    )
    mixed = jnp.dot(attended, w_out, preferred_element_type=jnp.float32).astype(jnp.bfloat16)
    return (mixed.reshape(sample_count, tokens_dev, model_width), new_centers)


def solution(mesh):
    return jax.shard_map(
        per_device,
        mesh=mesh,
        in_specs=(
            P("groups", "seq", None),
            P(),
            P(),
            P(),
            P(),
            P(),
            P(),
            P("groups", None, None, None),
            P(),
            P(),
        ),
        out_specs=(P("groups", "seq", None), P("groups", None, None, None)),
        check_vma=False,
    )
```

profile of v0, /device:TPU:0, one launch (start us, length us, event | category | flops | bytes accessed | tf_op | source)
XLA Modules:
  0.0 120.0 jit_solution(16905698591683552414)
XLA Ops:
  7.2 5.8 %convolution_add_fusion = f32[256,1152]{1,0:T(8,128)S(1)} fusion(bf16[256,3072]{1,0:T(8,128)(2,1)} %bitcast.143, bf16[3072,1152]{1,0:T(8,128)(2,1)} %param.13, f32[1152]{0:T(1024)} %param.14), kind=kOutput, calls=%fused_computation.24 | convolution fusion | flops 1812234240 | bytes 9835008 | tf_op jit(solution)/shard_map/dot_general | solution.py:25
  13.0 1.4 %copy.42 = f32[256,1152]{0,1:T(8,128)} copy(f32[256,1152]{1,0:T(8,128)S(1)} %convolution_add_fusion) | data formatting | bytes 2359296 | tf_op jit(solution)/shard_map/add | solution.py:25
  14.4 1.9 %reshape.48 = f32[2,128,3,3,128]{1,0,4,3,2:T(2,128)S(1)} reshape(f32[256,1152]{0,1:T(8,128)} %copy.42) | data formatting | bytes 2359296 | tf_op jit(solution)/shard_map/reshape | solution.py:26
  17.2 1.8 %slice_reduce_fusion = (f32[2,3,128]{0,2,1:T(8,128)}, f32[2,128,1,3,128]{1,0,4,3,2:T(2,128)}) fusion(f32[2,128,3,3,128]{1,0,4,3,2:T(2,128)S(1)} %reshape.48), kind=kLoop, calls=%fused_computation.64 | loop fusion | flops 97536 | bytes 789504 | tf_op jit(solution)/shard_map/reduce_sum | solution.py:38
  18.9 1.9 %copy.64 = f32[2,128,1,3,128]{4,1,3,0,2:T(8,128)} copy(f32[2,128,1,3,128]{1,0,4,3,2:T(2,128)} %get-tuple-element.119) | data formatting | bytes 786432
  22.5 2.6 %fusion.32 = (f32[2,3,128]{0,2,1:T(8,128)}, f32[2,128,3,128]{1,0,3,2:T(2,128)S(1)}, f32[2,3,128,128]{2,0,3,1:T(2,128)}) fusion(f32[128]{0:T(128)} %param.16, f32[2,128,3]{1,0,2:T(2,128)S(1)} %get-tuple-element.129, f32[2,128,3,3,128]{1,0,4,3,2:T(2,128)S(1)} %reshape.48, f32[128]{0:T(128)} %param.15, f32[2,128,3]{1,0,2:T(2,128)S(1)} %get-tuple-element.130), kind=kLoop, calls=%fused_computation.65 | loop fusion | flops 490752 | bytes 1583104 | tf_op jit(solution)/shard_map/reduce_sum | solution.py:38
  27.1 1.2 copy.43
  28.3 1.6 %copy.56 = f32[2,3,128]{2,0,1:T(2,128)} copy(f32[2,3,128]{0,2,1:T(8,128)} %get-tuple-element.114) | data formatting | bytes 6144 | tf_op jit(solution)/shard_map/reduce_sum | solution.py:38
  29.9 1.6 %copy.57 = f32[2,3,128]{2,0,1:T(2,128)} copy(f32[2,3,128]{0,2,1:T(8,128)} %get-tuple-element.118) | data formatting | bytes 6144 | tf_op jit(solution)/shard_map/reduce_sum | solution.py:38
  32.2 36.5 %psum.7 = f32[2,2,3,128]{3,0,2,1:T(2,128)} all-reduce(f32[2,2,3,128]{3,0,2,1:T(2,128)S(1)} %pad_maximum_fusion), channel_id=1, replica_groups=mesh['groups'=2,'seq'=16] {'seq'}, use_global_device_ids=true, to_apply=%region_10.11 | all-reduce | flops 1536 | bytes 12288 | tf_op jit(solution)/shard_map/psum | solution.py:39
  73.2 3.9 %reshape_reshape.7 = bf16[4,512,2,2,3,32]{1,0,5,4,3,2:T(4,128)(2,1)} reshape(bf16[2048,384]{0,1:T(8,128)(2,1)} %all-gather.2.cloned.1.call-done) | data formatting | bytes 3145728 | tf_op jit(solution)/shard_map/reshape;reshape | solution.py:91
  77.0 2.9 %copy.53 = bf16[4,512,2,2,3,32]{1,5,4,2,3,0:T(8,128)(2,1)} copy(bf16[4,512,2,2,3,32]{1,0,5,4,3,2:T(4,128)(2,1)} %reshape_reshape.7) | data formatting | bytes 3145728 | tf_op jit(solution)/shard_map/while | solution.py:94
  80.0 30.7 %while.14 = (s32[]{:T(128)}, f32[2,3,128]{2,1,0:T(4,128)S(1)}, f32[2,3,128]{2,1,0:T(4,128)S(1)}, f32[2,3,128,128]{3,2,1,0:T(8,128)S(1)}, pred[4,512]{1,0:T(4,128...) while((s32[]{:T(128)}, f32[2,3,128]{2,1,0:T(4,128)S(1)}, ...), condition=%wide.region_7.8_spmd, body=%wide.region_4.7_spmd.sunk | while | flops 1513293312 | bytes 13524605 | solution.py:94
  80.0 1.0 dynamic-slice_bitcast_fusion.2
  81.9 1.6 %bitcast_reduce_fusion.2 = (f32[2,3,128]{2,1,0:T(4,128)S(1)}, f32[2,3,512,128]{3,2,1,0:T(8,128)S(1)}) fusion(f32[2,3,128,128]{3,2,1,0:T(8,128)S(1)} %get-tuple-element.240, f32[3,512,2,128]{3,1,0,2:T(8,128)S(1)} %fusion.54, f32[2,3,128]{2,1,0:T(4,128)S(1)} %bitcast.140, pred[512]{0:T(512)(128)(4,1)S(1)} %dynamic-slice_reduce_fusion.2), kind=kOutput, calls=%fused_computation.3.clone.1 | convolution fusion | flops 605551872 | bytes 3545600 | tf_op jit(solution)/shard_map/while/body/eval_jaxpr/bhqd,bhsd->bhqs/dot_general | solution.py:64
  84.8 2.9 %fusion.57 = f32[2,3,128,128]{3,2,1,0:T(8,128)S(1)} fusion(f32[3,512,2,128]{3,1,0,2:T(8,128)S(1)} %fusion.56, f32[2,3,512,128]{3,2,1,0:T(8,128)S(1)} %get-tuple-element.205, f32[2,3,128]{2,1,0:T(4,128)S(1)} %bitcast.139, f32[2,3,128]{2,1,0:T(4,128)S(1)} %max.4, f32[2,3,128,128]{3,2,1,0:T(8,128)S(1)} %get-tuple-element.223, ...), kind=kOutput, calls=%fused_computation.9.clone.1 | convolution fusion | flops 604962816 | bytes 3941376 | tf_op jit(solution)/shard_map/while/body/eval_jaxpr/bhqs,bhsd->bhqd/dot_general | solution.py:74
  87.7 1.0 dynamic-slice_bitcast_fusion.2
  89.6 1.6 %bitcast_reduce_fusion.2 = (f32[2,3,128]{2,1,0:T(4,128)S(1)}, f32[2,3,512,128]{3,2,1,0:T(8,128)S(1)}) fusion(f32[2,3,128,128]{3,2,1,0:T(8,128)S(1)} %get-tuple-element.240, f32[3,512,2,128]{3,1,0,2:T(8,128)S(1)} %fusion.54, f32[2,3,128]{2,1,0:T(4,128)S(1)} %bitcast.140, pred[512]{0:T(512)(128)(4,1)S(1)} %dynamic-slice_reduce_fusion.2), kind=kOutput, calls=%fused_computation.3.clone.1 | convolution fusion | flops 605551872 | bytes 3545600 | tf_op jit(solution)/shard_map/while/body/eval_jaxpr/bhqd,bhsd->bhqs/dot_general | solution.py:64
  92.4 2.9 %fusion.57 = f32[2,3,128,128]{3,2,1,0:T(8,128)S(1)} fusion(f32[3,512,2,128]{3,1,0,2:T(8,128)S(1)} %fusion.56, f32[2,3,512,128]{3,2,1,0:T(8,128)S(1)} %get-tuple-element.205, f32[2,3,128]{2,1,0:T(4,128)S(1)} %bitcast.139, f32[2,3,128]{2,1,0:T(4,128)S(1)} %max.4, f32[2,3,128,128]{3,2,1,0:T(8,128)S(1)} %get-tuple-element.223, ...), kind=kOutput, calls=%fused_computation.9.clone.1 | convolution fusion | flops 604962816 | bytes 3941376 | tf_op jit(solution)/shard_map/while/body/eval_jaxpr/bhqs,bhsd->bhqd/dot_general | solution.py:74
  97.3 1.6 %bitcast_reduce_fusion.2 = (f32[2,3,128]{2,1,0:T(4,128)S(1)}, f32[2,3,512,128]{3,2,1,0:T(8,128)S(1)}) fusion(f32[2,3,128,128]{3,2,1,0:T(8,128)S(1)} %get-tuple-element.240, f32[3,512,2,128]{3,1,0,2:T(8,128)S(1)} %fusion.54, f32[2,3,128]{2,1,0:T(4,128)S(1)} %bitcast.140, pred[512]{0:T(512)(128)(4,1)S(1)} %dynamic-slice_reduce_fusion.2), kind=kOutput, calls=%fused_computation.3.clone.1 | convolution fusion | flops 605551872 | bytes 3545600 | tf_op jit(solution)/shard_map/while/body/eval_jaxpr/bhqd,bhsd->bhqs/dot_general | solution.py:64
  100.1 2.9 %fusion.57 = f32[2,3,128,128]{3,2,1,0:T(8,128)S(1)} fusion(f32[3,512,2,128]{3,1,0,2:T(8,128)S(1)} %fusion.56, f32[2,3,512,128]{3,2,1,0:T(8,128)S(1)} %get-tuple-element.205, f32[2,3,128]{2,1,0:T(4,128)S(1)} %bitcast.139, f32[2,3,128]{2,1,0:T(4,128)S(1)} %max.4, f32[2,3,128,128]{3,2,1,0:T(8,128)S(1)} %get-tuple-element.223, ...), kind=kOutput, calls=%fused_computation.9.clone.1 | convolution fusion | flops 604962816 | bytes 3941376 | tf_op jit(solution)/shard_map/while/body/eval_jaxpr/bhqs,bhsd->bhqd/dot_general | solution.py:74
  105.0 1.6 %bitcast_reduce_fusion.2 = (f32[2,3,128]{2,1,0:T(4,128)S(1)}, f32[2,3,512,128]{3,2,1,0:T(8,128)S(1)}) fusion(f32[2,3,128,128]{3,2,1,0:T(8,128)S(1)} %get-tuple-element.240, f32[3,512,2,128]{3,1,0,2:T(8,128)S(1)} %fusion.54, f32[2,3,128]{2,1,0:T(4,128)S(1)} %bitcast.140, pred[512]{0:T(512)(128)(4,1)S(1)} %dynamic-slice_reduce_fusion.2), kind=kOutput, calls=%fused_computation.3.clone.1 | convolution fusion | flops 605551872 | bytes 3545600 | tf_op jit(solution)/shard_map/while/body/eval_jaxpr/bhqd,bhsd->bhqs/dot_general | solution.py:64
  107.8 2.9 %fusion.57 = f32[2,3,128,128]{3,2,1,0:T(8,128)S(1)} fusion(f32[3,512,2,128]{3,1,0,2:T(8,128)S(1)} %fusion.56, f32[2,3,512,128]{3,2,1,0:T(8,128)S(1)} %get-tuple-element.205, f32[2,3,128]{2,1,0:T(4,128)S(1)} %bitcast.139, f32[2,3,128]{2,1,0:T(4,128)S(1)} %max.4, f32[2,3,128,128]{3,2,1,0:T(8,128)S(1)} %get-tuple-element.223, ...), kind=kOutput, calls=%fused_computation.9.clone.1 | convolution fusion | flops 604962816 | bytes 3941376 | tf_op jit(solution)/shard_map/while/body/eval_jaxpr/bhqs,bhsd->bhqd/dot_general | solution.py:74
  111.0 2.2 %convolution_convert_fusion = bf16[256,3072]{1,0:T(8,128)(2,1)} fusion(bf16[384,3072]{1,0:T(8,128)(2,1)S(1)} %copy-done, bf16[48,8,2,128]{3,2,1,0:T(2,128)(2,1)S(1)} %bitcast.137), kind=kOutput, calls=%fused_computation.23 | convolution fusion | flops 604766208 | bytes 4128768 | tf_op jit(solution)/shard_map/dot_general | solution.py:100
  (77 shorter events, 20.3 us)
Async XLA Ops:
  7.2 103.9 %copy-start = (bf16[384,3072]{1,0:T(8,128)(2,1)S(1)}, bf16[384,3072]{1,0:T(8,128)(2,1)}, u32[]{:S(2)}) copy-start(bf16[384,3072]{1,0:T(8,128)(2,1)} %param.21) | copy-start | bytes 7077892
  7.2 66.0 %all-gather.2.cloned.1.call-start = ((), (), s32[]{:S(2)}) async-start(), calls=%async_computation | async-start | bytes 1671168 | tf_op jit(solution)/shard_map/all_gather | solution.py:79
  16.3 4.6 %copy-start.11 = (f32[2,2,3,128]{3,1,2,0:T(2,128)S(1)}, f32[2,2,3,128]{3,1,2,0:T(2,128)}, u32[]{:S(2)}) copy-start(f32[2,2,3,128]{3,1,2,0:T(2,128)} %param.19) | copy-start | bytes 18436
  21.7 3.3 %copy-start.9 = (f32[2,3,128]{0,2,1:T(8,128)S(1)}, f32[2,3,128]{0,2,1:T(8,128)}, u32[]{:S(2)}) copy-start(f32[2,3,128]{0,2,1:T(8,128)} %copy.48) | copy-start | bytes 9220
  21.7 3.8 %copy-start.7 = (f32[3,128,32]{1,2,0:T(8,128)S(1)}, f32[3,128,32]{1,2,0:T(8,128)}, u32[]{:S(2)}) copy-start(f32[3,128,32]{1,2,0:T(8,128)} %param.17) | copy-start | bytes 147460
  22.4 3.4 %copy-start.1 = (f32[2,128,1,3,128]{4,1,3,0,2:T(8,128)S(1)}, f32[2,128,1,3,128]{4,1,3,0,2:T(8,128)}, u32[]{:S(2)}) copy-start(f32[2,128,1,3,128]{4,1,3,0,2:T(8,128)} %copy.64) | copy-start | bytes 1179652
  22.4 3.4 %copy-start.5 = (f32[3,128,32]{1,2,0:T(8,128)S(1)}, f32[3,128,32]{1,2,0:T(8,128)}, u32[]{:S(2)}) copy-start(f32[3,128,32]{1,2,0:T(8,128)} %param.18) | copy-start | bytes 147460
  25.0 1.4 %copy-start.3 = (f32[2,128,3,128]{1,0,3,2:T(2,128)}, f32[2,128,3,128]{1,0,3,2:T(2,128)S(1)}, u32[]{:S(2)}) copy-start(f32[2,128,3,128]{1,0,3,2:T(2,128)S(1)} %get-tuple-element.115) | copy-start | bytes 1179652
  26.4 45.0 %copy-start.4 = (f32[2,128,3,128]{1,0,3,2:T(2,128)S(1)}, f32[2,128,3,128]{1,0,3,2:T(2,128)}, u32[]{:S(2)}) copy-start(f32[2,128,3,128]{1,0,3,2:T(2,128)} %copy-done.3) | copy-start | bytes 1179652
  26.4 45.9 %copy-start.2 = (f32[2,128,1,3,128]{4,1,3,0,2:T(8,128)S(1)}, f32[2,128,1,3,128]{4,1,3,0,2:T(8,128)}, u32[]{:S(2)}) copy-start(f32[2,128,1,3,128]{4,1,3,0,2:T(8,128)} %copy.64) | copy-start | bytes 1179652
  77.0 2.9 %copy-start.6 = (f32[3,128,32]{1,2,0:T(8,128)S(1)}, f32[3,128,32]{1,2,0:T(8,128)}, u32[]{:S(2)}) copy-start(f32[3,128,32]{1,2,0:T(8,128)} %param.18) | copy-start | bytes 147460
  77.0 2.9 %copy-start.8 = (f32[3,128,32]{1,2,0:T(8,128)S(1)}, f32[3,128,32]{1,2,0:T(8,128)}, u32[]{:S(2)}) copy-start(f32[3,128,32]{1,2,0:T(8,128)} %param.17) | copy-start | bytes 147460
  77.0 2.9 %copy-start.10 = (pred[4,512]{1,0:T(4,128)(4,1)S(1)}, pred[4,512]{1,0:T(4,128)(4,1)}, u32[]{:S(2)}) copy-start(pred[4,512]{1,0:T(4,128)(4,1)} %fusion.31) | copy-start | bytes 6148
Sparse Core Ops, SparseCore 0:
  27.2 41.7 all-gather.1
where the time goes:
time: 121 us; the launch traced here: 120 us
  blocking collectives  36.5 us (30%)
  matrix products  35.6 us (29%)
  local copies, waits for them, and re-layouts  22.8 us (19%)
  between operations  14.3 us (12%)
  other arithmetic  10.5 us (9%)
    psum x1, blocking collectives, per_device(): summed = lax.psum(local_sums, 'seq')  36.5 us
    dot_general x4, matrix products, absorb(): jnp.einsum('bhqs,bhsd->bhqd', weights, value_rebuilt, precision=highest)  11.5 us
    dot_general x4, matrix products, absorb(): jnp.einsum('bhqd,bhsd->bhqs', query_heads, key_rebuilt, precision=highest)  6.57 us
    dot_general x1, matrix products, per_device(): jnp.dot(flat_images, w_qkv, preferred_element_type=jnp.float32) + b_qkv  5.77 us
    squeeze x4, local copies, waits for them, and re-layouts, per_device(): result, unused = lax.scan(advance, start_state, stacked)  4.1 us
    another operation x1, local copies, waits for them, and re-layouts, per_device(): code_block.reshape(block_count, block_rows, sample_count - 0, 2, head_cou...  3.85 us
    dot_general x4, matrix products, absorb(): jnp.einsum('sbhr,hdr->bhsd', key_part, key_basis, precision=highest)  3.58 us
    dot_general x4, matrix products, absorb(): jnp.einsum('sbhr,hdr->bhsd', value_part, value_basis, precision=highest)  3.56 us
  transfers between devices with their start and end apart: 1, of which 0 were waited for; matrix products, arithmetic and copies ran while one was open for 8% of the time, Pallas kernels for 0%

commit v1 on v0

--- a/solution.py
+++ b/solution.py
@@ -1,3 +1,4 @@
+import functools
 import math
 import jax
 import jax.numpy as jnp
@@ -6,6 +7,14 @@
 
 epsilon = 1e-06
 highest = lax.Precision.HIGHEST
+
+
+def manage_the_orders(matrix, shard_axis):
+    field_out = lax.all_gather(matrix, axis_name=shard_axis)
+    return jnp.sum(field_out, 0)
+
+
+numbers_push = functools.partial(manage_the_orders, shard_axis="seq")
 
 
 def normalize(values, gain):
@@ -36,7 +45,7 @@
         "bthd,hdr->bthr", values_local - value_center[:, None], value_basis, precision=highest
     ).astype(jnp.bfloat16)
     local_sums = jnp.stack([jnp.sum(keys_local, axis=1), jnp.sum(values_local, axis=1)], axis=1)
-    summed = lax.psum(local_sums, "seq")
+    summed = numbers_push(local_sums)
     fresh_means = summed / (tokens_dev * seq_count)
     new_centers = jnp.where(refresh[None, :, :, None] == 1, fresh_means, centers)
     query_heads = queries.transpose(0, 2, 1, 3)

time: 121 us -> 116 us (0.959)
  blocking collectives: 36.5 us -> 25.1 us
  waiting for transfers between devices: 0.04 us -> 6.75 us
    psum x1 -> x0, blocking collectives: 36.5 us -> none  [per_device(): summed = lax.psum(local_sums, 'seq')]
    all_gather x0 -> x1, blocking collectives: none -> 25.1 us  [manage_the_orders(): field_out = lax.all_gather(matrix, axis_name=shard_axis)]
    all_gather x1, waiting for transfers between devices: 0.02 us -> 6.73 us  [per_device(): shard_codes = lax.all_gather(whole_codes, 'seq', axis=0, tiled=True)]
    reduce_sum x2 -> x0, local copies, waits for them, and re-layouts: 3.22 us -> none  [the longest x1 1.61 us: per_device(): jnp.sum(keys_local, axis=1)]
    another operation x0 -> x2, local copies, waits for them, and re-layouts: none -> 1.62 us  [per_device(): jnp.stack([jnp.sum(keys_local, axis=1), jnp.sum(values_local, axis=1)], a...]
    unnamed x27 -> x28, local copies, waits for them, and re-layouts: 2.56 us -> 3.59 us
  transfers between devices with their start and end apart: 1 -> 1, of which waited for: 0 -> 1; matrix products, arithmetic and copies ran while one was open for 8% -> 9% of each run, Pallas kernels for 0% -> 0%
where the time goes in v1:
time: 116 us
  matrix products  35.6 us (31%)
  blocking collectives  25.1 us (22%)
  local copies, waits for them, and re-layouts  22.3 us (19%)
  between operations  14.2 us (12%)
  other arithmetic  11.4 us (10%)
  waiting for transfers between devices  6.75 us (6%)
    all_gather x1, blocking collectives, manage_the_orders(): field_out = lax.all_gather(matrix, axis_name=shard_axis)  25.1 us
    dot_general x4, matrix products, absorb(): jnp.einsum('bhqs,bhsd->bhqd', weights, value_rebuilt, precision=highest)  11.5 us
    all_gather x1, waiting for transfers between devices, per_device(): shard_codes = lax.all_gather(whole_codes, 'seq', axis=0, tiled=True)  6.73 us
    dot_general x4, matrix products, absorb(): jnp.einsum('bhqd,bhsd->bhqs', query_heads, key_rebuilt, precision=highest)  6.58 us
    dot_general x1, matrix products, per_device(): jnp.dot(flat_images, w_qkv, preferred_element_type=jnp.float32) + b_qkv  5.77 us
    squeeze x4, local copies, waits for them, and re-layouts, per_device(): result, unused = lax.scan(advance, start_state, stacked)  4.1 us
    another operation x1, local copies, waits for them, and re-layouts, per_device(): code_block.reshape(block_count, block_rows, sample_count - 0, 2, head_cou...  3.85 us
    unnamed x28, local copies, waits for them, and re-layouts  3.59 us
  transfers between devices with their start and end apart: 1, of which 1 were waited for; matrix products, arithmetic and copies ran while one was open for 9% of the time, Pallas kernels for 0%

profile of v1, /device:TPU:0, one launch (start us, length us, event | category | flops | bytes accessed | tf_op | source)
XLA Modules:
  0.0 115.7 jit_solution(16703067394438944353)
XLA Ops:
  7.2 5.8 %convolution_add_fusion = f32[256,1152]{1,0:T(8,128)S(1)} fusion(bf16[256,3072]{1,0:T(8,128)(2,1)} %bitcast.147, bf16[3072,1152]{1,0:T(8,128)(2,1)} %param.13, f32[1152]{0:T(1024)} %param.14), kind=kOutput, calls=%fused_computation.24 | convolution fusion | flops 1812234240 | bytes 9835008 | tf_op jit(solution)/shard_map/dot_general | solution.py:34
  13.0 1.4 %copy.74 = f32[256,1152]{0,1:T(8,128)} copy(f32[256,1152]{1,0:T(8,128)S(1)} %convolution_add_fusion) | data formatting | bytes 2359296 | tf_op jit(solution)/shard_map/add | solution.py:34
  14.4 1.9 %reshape.48 = f32[2,128,3,3,128]{1,0,4,3,2:T(2,128)S(1)} reshape(f32[256,1152]{0,1:T(8,128)} %copy.74) | data formatting | bytes 2359296 | tf_op jit(solution)/shard_map/reshape | solution.py:35
  17.2 1.8 %slice_reduce_fusion = (f32[2,3,128]{0,2,1:T(8,128)}, f32[2,128,1,3,128]{1,0,4,3,2:T(2,128)}) fusion(f32[2,128,3,3,128]{1,0,4,3,2:T(2,128)S(1)} %reshape.48), kind=kLoop, calls=%fused_computation.65 | loop fusion | flops 97536 | bytes 789504 | tf_op jit(solution)/shard_map/reduce_sum | solution.py:47
  18.9 1.9 %copy.98 = f32[2,128,1,3,128]{4,1,3,0,2:T(8,128)} copy(f32[2,128,1,3,128]{1,0,4,3,2:T(2,128)} %get-tuple-element.139) | data formatting | bytes 786432
  22.5 2.6 %fusion.33 = (f32[2,3,128]{0,2,1:T(8,128)}, f32[2,128,3,128]{1,0,3,2:T(2,128)S(1)}, f32[2,3,128,128]{2,0,3,1:T(2,128)}) fusion(f32[128]{0:T(128)} %param.16, f32[2,128,3]{1,0,2:T(2,128)S(1)} %get-tuple-element.149, f32[2,128,3,3,128]{1,0,4,3,2:T(2,128)S(1)} %reshape.48, f32[128]{0:T(128)} %param.15, f32[2,128,3]{1,0,2:T(2,128)S(1)} %get-tuple-element.150), kind=kLoop, calls=%fused_computation.66 | loop fusion | flops 490752 | bytes 1583104 | tf_op jit(solution)/shard_map/reduce_sum | solution.py:47
  27.1 1.2 %copy.75 = f32[2,3,128,128]{3,2,1,0:T(8,128)S(1)} copy(f32[2,3,128,128]{2,0,3,1:T(2,128)} %get-tuple-element.140) | data formatting | bytes 786432 | tf_op jit(solution)/shard_map/transpose | solution.py:51
  28.3 1.6 %copy.88 = f32[2,1,3,128]{3,1,2,0:T(1,128)} copy(f32[2,1,3,128]{0,3,2,1:T(8,128)} %bitcast.141) | data formatting | bytes 6144 | tf_op jit(solution)/shard_map/stack | solution.py:47
  29.9 1.0 copy.101
  31.7 25.1 %all-gather = f32[32,2,3,128]{3,1,2,0:T(2,128)} all-gather(f32[2,2,3,128]{3,1,2,0:T(2,128)S(1)} %pad_maximum_fusion), channel_id=2, replica_groups=mesh['groups'=2,'seq'=16] {'seq'}, dimensions={0}, use_global_device_ids=true | all-gather | bytes 104448 | tf_op jit(solution)/shard_map/all_gather | solution.py:13
  62.1 6.7 %all-gather.3.cloned.1.call-done = bf16[2048,384]{0,1:T(8,128)(2,1)} async-done(((bf16[128,384]{0,1:T(8,128)(2,1)}), bf16[2048,384]{0,1:T(8,128)(2,1)}) %all-gather.3.cloned.1.call-update) | async-done | bytes 1572880 | tf_op jit(solution)/shard_map/all_gather | solution.py:88
  68.8 3.8 %reshape_reshape.7 = bf16[4,512,2,2,3,32]{1,0,5,4,3,2:T(4,128)(2,1)} reshape(bf16[2048,384]{0,1:T(8,128)(2,1)} %all-gather.3.cloned.1.call-done) | data formatting | bytes 3145728 | tf_op jit(solution)/shard_map/reshape;reshape | solution.py:100
  72.6 2.9 %copy.85 = bf16[4,512,2,2,3,32]{1,5,4,2,3,0:T(8,128)(2,1)} copy(bf16[4,512,2,2,3,32]{1,0,5,4,3,2:T(4,128)(2,1)} %reshape_reshape.7) | data formatting | bytes 3145728 | tf_op jit(solution)/shard_map/while | solution.py:103
  75.6 30.7 %while.14 = (s32[]{:T(128)}, f32[2,3,128]{2,1,0:T(4,128)S(1)}, f32[2,3,128]{2,1,0:T(4,128)S(1)}, f32[2,3,128,128]{3,2,1,0:T(8,128)S(1)}, pred[4,512]{1,0:T(4,128...) while((s32[]{:T(128)}, f32[2,3,128]{2,1,0:T(4,128)S(1)}, ...), condition=%wide.region_7.8_spmd, body=%wide.region_4.7_spmd.sunk | while | flops 1513293312 | bytes 13524605 | solution.py:103
  77.6 1.6 %bitcast_reduce_fusion.2 = (f32[2,3,128]{2,1,0:T(4,128)S(1)}, f32[2,3,512,128]{3,2,1,0:T(8,128)S(1)}) fusion(f32[2,3,128,128]{3,2,1,0:T(8,128)S(1)} %get-tuple-element.260, f32[3,512,2,128]{3,1,0,2:T(8,128)S(1)} %fusion.55, f32[2,3,128]{2,1,0:T(4,128)S(1)} %bitcast.145, pred[512]{0:T(512)(128)(4,1)S(1)} %dynamic-slice_reduce_fusion.2), kind=kOutput, calls=%fused_computation.3.clone.1 | convolution fusion | flops 605551872 | bytes 3545600 | tf_op jit(solution)/shard_map/while/body/eval_jaxpr/bhqd,bhsd->bhqs/dot_general | solution.py:73
  80.4 2.9 %fusion.58 = f32[2,3,128,128]{3,2,1,0:T(8,128)S(1)} fusion(f32[3,512,2,128]{3,1,0,2:T(8,128)S(1)} %fusion.57, f32[2,3,512,128]{3,2,1,0:T(8,128)S(1)} %get-tuple-element.225, f32[2,3,128]{2,1,0:T(4,128)S(1)} %bitcast.144, f32[2,3,128]{2,1,0:T(4,128)S(1)} %max.4, f32[2,3,128,128]{3,2,1,0:T(8,128)S(1)} %get-tuple-element.243, ...), kind=kOutput, calls=%fused_computation.9.clone.1 | convolution fusion | flops 604962816 | bytes 3941376 | tf_op jit(solution)/shard_map/while/body/eval_jaxpr/bhqs,bhsd->bhqd/dot_general | solution.py:83
  83.3 1.0 dynamic-slice_bitcast_fusion.2
  85.2 1.6 %bitcast_reduce_fusion.2 = (f32[2,3,128]{2,1,0:T(4,128)S(1)}, f32[2,3,512,128]{3,2,1,0:T(8,128)S(1)}) fusion(f32[2,3,128,128]{3,2,1,0:T(8,128)S(1)} %get-tuple-element.260, f32[3,512,2,128]{3,1,0,2:T(8,128)S(1)} %fusion.55, f32[2,3,128]{2,1,0:T(4,128)S(1)} %bitcast.145, pred[512]{0:T(512)(128)(4,1)S(1)} %dynamic-slice_reduce_fusion.2), kind=kOutput, calls=%fused_computation.3.clone.1 | convolution fusion | flops 605551872 | bytes 3545600 | tf_op jit(solution)/shard_map/while/body/eval_jaxpr/bhqd,bhsd->bhqs/dot_general | solution.py:73
  88.1 2.9 %fusion.58 = f32[2,3,128,128]{3,2,1,0:T(8,128)S(1)} fusion(f32[3,512,2,128]{3,1,0,2:T(8,128)S(1)} %fusion.57, f32[2,3,512,128]{3,2,1,0:T(8,128)S(1)} %get-tuple-element.225, f32[2,3,128]{2,1,0:T(4,128)S(1)} %bitcast.144, f32[2,3,128]{2,1,0:T(4,128)S(1)} %max.4, f32[2,3,128,128]{3,2,1,0:T(8,128)S(1)} %get-tuple-element.243, ...), kind=kOutput, calls=%fused_computation.9.clone.1 | convolution fusion | flops 604962816 | bytes 3941376 | tf_op jit(solution)/shard_map/while/body/eval_jaxpr/bhqs,bhsd->bhqd/dot_general | solution.py:83
  92.9 1.6 %bitcast_reduce_fusion.2 = (f32[2,3,128]{2,1,0:T(4,128)S(1)}, f32[2,3,512,128]{3,2,1,0:T(8,128)S(1)}) fusion(f32[2,3,128,128]{3,2,1,0:T(8,128)S(1)} %get-tuple-element.260, f32[3,512,2,128]{3,1,0,2:T(8,128)S(1)} %fusion.55, f32[2,3,128]{2,1,0:T(4,128)S(1)} %bitcast.145, pred[512]{0:T(512)(128)(4,1)S(1)} %dynamic-slice_reduce_fusion.2), kind=kOutput, calls=%fused_computation.3.clone.1 | convolution fusion | flops 605551872 | bytes 3545600 | tf_op jit(solution)/shard_map/while/body/eval_jaxpr/bhqd,bhsd->bhqs/dot_general | solution.py:73
  95.7 2.9 %fusion.58 = f32[2,3,128,128]{3,2,1,0:T(8,128)S(1)} fusion(f32[3,512,2,128]{3,1,0,2:T(8,128)S(1)} %fusion.57, f32[2,3,512,128]{3,2,1,0:T(8,128)S(1)} %get-tuple-element.225, f32[2,3,128]{2,1,0:T(4,128)S(1)} %bitcast.144, f32[2,3,128]{2,1,0:T(4,128)S(1)} %max.4, f32[2,3,128,128]{3,2,1,0:T(8,128)S(1)} %get-tuple-element.243, ...), kind=kOutput, calls=%fused_computation.9.clone.1 | convolution fusion | flops 604962816 | bytes 3941376 | tf_op jit(solution)/shard_map/while/body/eval_jaxpr/bhqs,bhsd->bhqd/dot_general | solution.py:83
  100.6 1.6 %bitcast_reduce_fusion.2 = (f32[2,3,128]{2,1,0:T(4,128)S(1)}, f32[2,3,512,128]{3,2,1,0:T(8,128)S(1)}) fusion(f32[2,3,128,128]{3,2,1,0:T(8,128)S(1)} %get-tuple-element.260, f32[3,512,2,128]{3,1,0,2:T(8,128)S(1)} %fusion.55, f32[2,3,128]{2,1,0:T(4,128)S(1)} %bitcast.145, pred[512]{0:T(512)(128)(4,1)S(1)} %dynamic-slice_reduce_fusion.2), kind=kOutput, calls=%fused_computation.3.clone.1 | convolution fusion | flops 605551872 | bytes 3545600 | tf_op jit(solution)/shard_map/while/body/eval_jaxpr/bhqd,bhsd->bhqs/dot_general | solution.py:73
  103.4 2.9 %fusion.58 = f32[2,3,128,128]{3,2,1,0:T(8,128)S(1)} fusion(f32[3,512,2,128]{3,1,0,2:T(8,128)S(1)} %fusion.57, f32[2,3,512,128]{3,2,1,0:T(8,128)S(1)} %get-tuple-element.225, f32[2,3,128]{2,1,0:T(4,128)S(1)} %bitcast.144, f32[2,3,128]{2,1,0:T(4,128)S(1)} %max.4, f32[2,3,128,128]{3,2,1,0:T(8,128)S(1)} %get-tuple-element.243, ...), kind=kOutput, calls=%fused_computation.9.clone.1 | convolution fusion | flops 604962816 | bytes 3941376 | tf_op jit(solution)/shard_map/while/body/eval_jaxpr/bhqs,bhsd->bhqd/dot_general | solution.py:83
  106.7 2.2 %convolution_convert_fusion = bf16[256,3072]{1,0:T(8,128)(2,1)} fusion(bf16[384,3072]{1,0:T(8,128)(2,1)S(1)} %copy-done, bf16[48,8,2,128]{3,2,1,0:T(2,128)(2,1)S(1)} %bitcast.140), kind=kOutput, calls=%fused_computation.23 | convolution fusion | flops 604766208 | bytes 4128768 | tf_op jit(solution)/shard_map/dot_general | solution.py:109
  (79 shorter events, 22.3 us)
Async XLA Ops:
  7.2 99.5 %copy-start = (bf16[384,3072]{1,0:T(8,128)(2,1)S(1)}, bf16[384,3072]{1,0:T(8,128)(2,1)}, u32[]{:S(2)}) copy-start(bf16[384,3072]{1,0:T(8,128)(2,1)} %param.21) | copy-start | bytes 7077892
  7.2 61.6 %all-gather.3.cloned.1.call-start = ((), (), s32[]{:S(2)}) async-start(), calls=%async_computation | async-start | bytes 1671168 | tf_op jit(solution)/shard_map/all_gather | solution.py:88
  16.3 4.6 %copy-start.11 = (f32[2,2,3,128]{3,1,2,0:T(2,128)S(1)}, f32[2,2,3,128]{3,1,2,0:T(2,128)}, u32[]{:S(2)}) copy-start(f32[2,2,3,128]{3,1,2,0:T(2,128)} %param.19) | copy-start | bytes 18436
  21.7 3.3 %copy-start.9 = (f32[2,3,128]{0,2,1:T(8,128)S(1)}, f32[2,3,128]{0,2,1:T(8,128)}, u32[]{:S(2)}) copy-start(f32[2,3,128]{0,2,1:T(8,128)} %copy.80) | copy-start | bytes 9220
  21.7 3.8 %copy-start.7 = (f32[3,128,32]{1,2,0:T(8,128)S(1)}, f32[3,128,32]{1,2,0:T(8,128)}, u32[]{:S(2)}) copy-start(f32[3,128,32]{1,2,0:T(8,128)} %param.17) | copy-start | bytes 147460
  22.4 3.4 %copy-start.1 = (f32[2,128,1,3,128]{4,1,3,0,2:T(8,128)S(1)}, f32[2,128,1,3,128]{4,1,3,0,2:T(8,128)}, u32[]{:S(2)}) copy-start(f32[2,128,1,3,128]{4,1,3,0,2:T(8,128)} %copy.98) | copy-start | bytes 1179652
  22.4 3.4 %copy-start.5 = (f32[3,128,32]{1,2,0:T(8,128)S(1)}, f32[3,128,32]{1,2,0:T(8,128)}, u32[]{:S(2)}) copy-start(f32[3,128,32]{1,2,0:T(8,128)} %param.18) | copy-start | bytes 147460
  25.0 1.4 %copy-start.3 = (f32[2,128,3,128]{1,0,3,2:T(2,128)}, f32[2,128,3,128]{1,0,3,2:T(2,128)S(1)}, u32[]{:S(2)}) copy-start(f32[2,128,3,128]{1,0,3,2:T(2,128)S(1)} %get-tuple-element.135) | copy-start | bytes 1179652
  26.4 33.9 %copy-start.4 = (f32[2,128,3,128]{1,0,3,2:T(2,128)S(1)}, f32[2,128,3,128]{1,0,3,2:T(2,128)}, u32[]{:S(2)}) copy-start(f32[2,128,3,128]{1,0,3,2:T(2,128)} %copy-done.3) | copy-start | bytes 1179652
  27.1 34.2 %copy-start.2 = (f32[2,128,1,3,128]{4,1,3,0,2:T(8,128)S(1)}, f32[2,128,1,3,128]{4,1,3,0,2:T(8,128)}, u32[]{:S(2)}) copy-start(f32[2,128,1,3,128]{4,1,3,0,2:T(8,128)} %copy.98) | copy-start | bytes 1179652
  72.6 2.9 %copy-start.6 = (f32[3,128,32]{1,2,0:T(8,128)S(1)}, f32[3,128,32]{1,2,0:T(8,128)}, u32[]{:S(2)}) copy-start(f32[3,128,32]{1,2,0:T(8,128)} %param.18) | copy-start | bytes 147460
  72.6 2.9 %copy-start.8 = (f32[3,128,32]{1,2,0:T(8,128)S(1)}, f32[3,128,32]{1,2,0:T(8,128)}, u32[]{:S(2)}) copy-start(f32[3,128,32]{1,2,0:T(8,128)} %param.17) | copy-start | bytes 147460
  72.6 2.9 %copy-start.10 = (pred[4,512]{1,0:T(4,128)(4,1)S(1)}, pred[4,512]{1,0:T(4,128)(4,1)}, u32[]{:S(2)}) copy-start(pred[4,512]{1,0:T(4,128)(4,1)} %fusion.31) | copy-start | bytes 6148
Sparse Core Ops, SparseCore 0:
  27.2 41.5 all-gather.2
